TPU v7x, 32 devices: a whole 2x2x4 slice. The times are simulated.
32 devices in a mesh: feat: 2 (over x), lat: 16 (over z, y, core).
Axes of the slice: x: 2, y: 2, z: 4, core: 2. Of those that a mesh axis runs over, the one named last changes fastest.
Arguments:
- acts: bfloat16 [2, 128, 4096], P(None, 'lat', 'feat'), may hold values from -6 to 6
- weight: bfloat16 [2, 4096, 16384], P(None, 'feat', 'lat'), may hold values from -0.0625 to 0.0625
- enc_bias: float32 [16384], P('lat'), may hold values from -1 to 0.5
- dec_bias: float32 [2, 4096], P(None, 'feat'), may hold values from -1 to 1
Outputs:
- grad_weight: bfloat16 [2, 4096, 16384], P(None, 'feat', 'lat')
- grad_enc_bias: float32 [16384], P('lat')
- grad_dec_bias: float32 [2, 4096], P(None, 'feat')
All inputs are finite; a program needn't handle non-finite values.
Results may differ from a plain program's by a relative error of at most 0.0085.
Values may be sent and summed in bfloat16 or wider, within the bound.
No kernel may reach another device: no remote copies, remote signals or barrier semaphores. Data moves between devices by JAX's collectives and lax.ppermute only.
A program may use at most 128 MiB of HBM per device.

v0:
```python
import math
import jax
import jax.numpy as jnp
from jax import lax
from jax.sharding import PartitionSpec as P


def channel_terms(left, right):
    first = jnp.dot(left[0], right[0], preferred_element_type=jnp.float32)
    return first + jnp.dot(left[1], right[1], preferred_element_type=jnp.float32)


def on_device(acts, weight, enc_bias, dec_bias):
    width = weight.shape[1] * lax.axis_size("feat")
    lats = weight.shape[2] * lax.axis_size("lat")
    scale = math.sqrt(2.0 * width / lats)
    whole_rows = lax.all_gather(acts, "lat", axis=1, tiled=True)
    partial_value = channel_terms(whole_rows, weight)
    pre_share = (
        lax.psum_scatter(
            partial_value.astype(jnp.bfloat16), "feat", scatter_dimension=0, tiled=True
        ).astype(jnp.float32)
        + enc_bias
    )
    act_share = jax.nn.softplus(pre_share).astype(jnp.bfloat16)
    latents = lax.all_gather(act_share, "feat", axis=0, tiled=True)
    recon_terms = jnp.einsum("rl,mdl->mrd", latents, weight, preferred_element_type=jnp.float32)
    summed = lax.psum(recon_terms, "lat")
    resid = scale * summed + dec_bias[:, None, :] - whole_rows.astype(jnp.float32)
    grad_dec_bias = jnp.sum(resid, axis=1)
    resid_rows = resid.astype(jnp.bfloat16)
    backed = channel_terms(resid_rows, weight)
    back_part = lax.psum_scatter(
        backed.astype(jnp.bfloat16), "feat", scatter_dimension=0, tiled=True
    ).astype(jnp.float32)
    grad_share = scale * back_part * jax.nn.sigmoid(pre_share)
    grad_enc_bias = lax.psum(jnp.sum(grad_share, axis=0), "feat")
    grad_pre_b = lax.all_gather(grad_share.astype(jnp.bfloat16), "feat", axis=0, tiled=True)
    enc_term = jnp.einsum("mrd,rl->mdl", whole_rows, grad_pre_b, preferred_element_type=jnp.float32)
    dec_term = jnp.einsum("mrd,rl->mdl", resid_rows, latents, preferred_element_type=jnp.float32)
    grad_weight = (enc_term + scale * dec_term).astype(jnp.bfloat16)
    return (grad_weight, grad_enc_bias, grad_dec_bias)


def solution(mesh):
    placed = (P(None, "lat", "feat"), P(None, "feat", "lat"), P("lat"), P(None, "feat"))
    return jax.shard_map(
        on_device,
        mesh=mesh,
        in_specs=placed,
        out_specs=(P(None, "feat", "lat"), P("lat"), P(None, "feat")),
        check_vma=False,
    )
```

profile of v0, /device:TPU:0, one launch (start us, length us, event | category | flops | bytes accessed | tf_op | source)
XLA Modules:
  0.0 249.5 jit_solution(9672463318507042027)
XLA Ops:
  7.2 0.0 copy-start.3
  7.2 0.0 all-gather.2.cloned.1.call-start
  7.2 0.7 all-gather.2.cloned.1.call-update
  7.9 0.0 reduce-scatter.3.cloned.1.call-start
  8.0 42.8 %all-gather.2.cloned.1.call-done = bf16[2,128,2048]{2,1,0:T(8,128)(2,1)} async-done(((bf16[2,8,2048]{2,1,0:T(8,128)(2,1)}), bf16[2,128,2048]{2,1,0:T(8,128)(2,1)}) %all-gather.2.cloned.1.call-update) | async-done | bytes 1048592 | tf_op jit(solution)/shard_map/all_gather | solution.py:17
  50.8 3.1 %fusion.3 = f32[128,1024]{1,0:T(8,128)S(1)} fusion(bf16[2,2048,1024]{2,1,0:T(8,128)(2,1)} %param.5, bf16[2,128,2048]{2,1,0:T(8,128)(2,1)} %all-gather.2.cloned.1.call-done), kind=kOutput, calls=%fused_computation.4 | convolution fusion | flops 536870912 | bytes 5242880 | tf_op jit(solution)/shard_map/dot_general | solution.py:10
  53.9 3.8 %fusion.22 = bf16[128,1024]{1,0:T(8,128)(2,1)} fusion(f32[128,1024]{1,0:T(8,128)S(1)} %fusion.3, bf16[2,2048,1024]{2,1,0:T(8,128)(2,1)} %param.5, bf16[2,128,2048]{2,1,0:T(8,128)(2,1)} %all-gather.2.cloned.1.call-done), kind=kOutput, calls=%fused_computation.19 | convolution fusion | flops 537133056 | bytes 5505024 | tf_op jit(solution)/shard_map/dot_general | solution.py:9
  57.6 0.0 copy-start
  57.7 0.0 copy-start.2
  57.7 0.0 reduce-scatter.3.cloned.1.call-update
  57.7 0.0 all-reduce.2.cloned.1.call-start
  57.7 10.8 %reduce-scatter.3.cloned.1.call-done = bf16[64,1024]{1,0:T(8,128)(2,1)} async-done(((bf16[128,1024]{1,0:T(8,128)(2,1)}), bf16[64,1024]{1,0:T(8,128)(2,1)}) %reduce-scatter.3.cloned.1.call-update) | async-done | bytes 131088 | tf_op jit(solution)/shard_map/reduce_scatter | solution.py:20
  68.6 0.0 copy-done.3
  68.6 1.1 fusion.27
  69.6 5.7 %all_gather.10 = bf16[128,1024]{1,0:T(8,128)(2,1)S(1)} all-gather(bf16[64,1024]{1,0:T(8,128)(2,1)S(1)} %fusion.27), channel_id=1, replica_groups=mesh['feat'=2,'lat'=16] {'feat'}, dimensions={0}, use_global_device_ids=true | all-gather | bytes 393216 | tf_op jit(solution)/shard_map/all_gather | solution.py:26
  75.4 7.6 %convolution_bitcast_fusion = f32[2,128,2048]{2,1,0:T(8,128)} fusion(bf16[2,2048,1024]{2,1,0:T(8,128)(2,1)} %param.5, bf16[128,1024]{1,0:T(8,128)(2,1)S(1)} %all_gather.10), kind=kOutput, calls=%fused_computation.14 | convolution fusion | flops 1073741824 | bytes 10747904 | tf_op jit(solution)/shard_map/rl,mdl->mrd/dot_general | solution.py:27
  82.9 0.0 all-reduce.2.cloned.1.call-update
  82.9 0.0 copy-start.1
  83.0 0.0 reduce-scatter.5.cloned.1.call-start
  83.0 98.1 %all-reduce.2.cloned.1.call-done = f32[2,128,2048]{2,1,0:T(8,128)} async-done(((f32[2,128,2048]{2,1,0:T(8,128)}), f32[2,128,2048]{2,1,0:T(8,128)}) %all-reduce.2.cloned.1.call-update) | async-done | bytes 2097168 | tf_op jit(solution)/shard_map/psum | solution.py:28
  181.1 0.0 copy-done
  181.1 0.0 copy-done.2
  181.1 2.6 %fusion.25 = (f32[2,2048]{1,0:T(2,128)}, bf16[2,128,2048]{2,1,0:T(8,128)(2,1)S(1)}) fusion(bf16[2,128,2048]{2,1,0:T(8,128)(2,1)S(1)} %copy-done, f32[2,128,2048]{2,1,0:T(8,128)} %all-reduce.2.cloned.1.call-done, f32[2,2048]{1,0:T(2,128)S(1)} %copy-done.2), kind=kLoop, calls=%fused_computation.20 | loop fusion | flops 3141632 | bytes 4227072 | tf_op jit(solution)/shard_map/reduce_sum | solution.py:30
  183.8 2.9 %fusion.1 = f32[128,1024]{1,0:T(8,128)S(1)} fusion(bf16[2,2048,1024]{2,1,0:T(8,128)(2,1)} %param.5, bf16[2,128,2048]{2,1,0:T(8,128)(2,1)S(1)} %get-tuple-element.7), kind=kOutput, calls=%fused_computation.2 | convolution fusion | flops 536870912 | bytes 5242880 | tf_op jit(solution)/shard_map/dot_general | solution.py:10
  186.7 3.6 %fusion.19 = bf16[128,1024]{1,0:T(8,128)(2,1)} fusion(f32[128,1024]{1,0:T(8,128)S(1)} %fusion.1, bf16[2,2048,1024]{2,1,0:T(8,128)(2,1)} %param.5, bf16[2,128,2048]{2,1,0:T(8,128)(2,1)S(1)} %get-tuple-element.7), kind=kOutput, calls=%fused_computation.18 | convolution fusion | flops 537133056 | bytes 5505024 | tf_op jit(solution)/shard_map/dot_general | solution.py:9
  190.3 0.0 reduce-scatter.5.cloned.1.call-update
  190.3 11.4 %reduce-scatter.5.cloned.1.call-done = bf16[64,1024]{1,0:T(8,128)(2,1)} async-done(((bf16[128,1024]{1,0:T(8,128)(2,1)}), bf16[64,1024]{1,0:T(8,128)(2,1)}) %reduce-scatter.5.cloned.1.call-update) | async-done | bytes 131088 | tf_op jit(solution)/shard_map/reduce_scatter | solution.py:33
  201.7 0.0 copy-done.1
  201.7 1.0 fusion.32
  202.7 5.5 %psum.15 = f32[1024]{0:T(1024)} all-reduce(f32[1024]{0:T(1024)S(1)} %get-tuple-element.8), channel_id=1, replica_groups=mesh['feat'=2,'lat'=16] {'feat'}, use_global_device_ids=true, to_apply=%region_4.5 | all-reduce | flops 1024 | bytes 8192 | tf_op jit(solution)/shard_map/psum | solution.py:37
  208.2 5.6 %all_gather.11 = bf16[128,1024]{1,0:T(8,128)(2,1)S(1)} all-gather(bf16[64,1024]{1,0:T(8,128)(2,1)S(1)} %get-tuple-element.9), channel_id=1, replica_groups=mesh['feat'=2,'lat'=16] {'feat'}, dimensions={0}, use_global_device_ids=true | all-gather | bytes 393216 | tf_op jit(solution)/shard_map/all_gather | solution.py:38
  213.9 8.1 %fusion.28 = f32[1024,2,2048]{2,0,1:T(8,128)} fusion(bf16[2,128,2048]{2,1,0:T(8,128)(2,1)S(1)} %copy-done, bf16[128,1024]{1,0:T(8,128)(2,1)S(1)} %all_gather.11), kind=kOutput, calls=%fused_computation.28 | convolution fusion | flops 1073741824 | bytes 18087936 | tf_op jit(solution)/shard_map/mrd,rl->mdl/dot_general | solution.py:39
  222.0 9.2 %fusion = bf16[2,2048,1024]{1,2,0:T(8,128)(2,1)} fusion(f32[1024,2,2048]{2,0,1:T(8,128)} %fusion.28, bf16[2,128,2048]{2,1,0:T(8,128)(2,1)S(1)} %get-tuple-element.7, bf16[128,1024]{1,0:T(8,128)(2,1)S(1)} %all_gather.10), kind=kOutput, calls=%fused_computation.1 | convolution fusion | flops 1086324736 | bytes 26476544 | tf_op jit(solution)/shard_map/mrd,rl->mdl/dot_general | solution.py:40
  231.2 11.8 %copy.9 = bf16[2,2048,1024]{2,1,0:T(8,128)(2,1)} copy(bf16[2,2048,1024]{1,2,0:T(8,128)(2,1)} %fusion) | data formatting | bytes 16777216
Async XLA Ops:
  7.2 61.4 %copy-start.3 = (f32[1024]{0:T(1024)S(1)}, f32[1024]{0:T(1024)}, u32[]{:S(2)}) copy-start(f32[1024]{0:T(1024)} %param.6) | copy-start | bytes 12292
  7.2 43.6 %all-gather.2.cloned.1.call-start = ((), (), s32[]{:S(2)}) async-start(), calls=%async_computation.2 | async-start | bytes 1114112 | tf_op jit(solution)/shard_map/all_gather | solution.py:17
  7.9 60.7 %reduce-scatter.3.cloned.1.call-start = ((), (), s32[]{:S(2)}) async-start(), calls=%async_computation.3 | async-start | bytes 393216 | tf_op jit(solution)/shard_map/reduce_scatter | solution.py:20
  57.6 123.5 %copy-start = (bf16[2,128,2048]{2,1,0:T(8,128)(2,1)S(1)}, bf16[2,128,2048]{2,1,0:T(8,128)(2,1)}, u32[]{:S(2)}) copy-start(bf16[2,128,2048]{2,1,0:T(8,128)(2,1)} %all-gather.2.cloned.1.call-done) | copy-start | bytes 3145732
  57.7 123.5 %copy-start.2 = (f32[2,2048]{1,0:T(2,128)S(1)}, f32[2,2048]{1,0:T(2,128)}, u32[]{:S(2)}) copy-start(f32[2,2048]{1,0:T(2,128)} %param.7) | copy-start | bytes 49156
  57.7 123.5 %all-reduce.2.cloned.1.call-start = ((), (), s32[]{:S(2)}) async-start(), calls=%async_computation.4 | async-start | bytes 4194304 | tf_op jit(solution)/shard_map/psum | solution.py:28
  82.9 118.8 %copy-start.1 = (bf16[64,1024]{1,0:T(8,128)(2,1)S(1)}, bf16[64,1024]{1,0:T(8,128)(2,1)}, u32[]{:S(2)}) copy-start(bf16[64,1024]{1,0:T(8,128)(2,1)} %reduce-scatter.3.cloned.1.call-done) | copy-start | bytes 393220
  83.0 118.8 %reduce-scatter.5.cloned.1.call-start = ((), (), s32[]{:S(2)}) async-start(), calls=%async_computation.5 | async-start | bytes 393216 | tf_op jit(solution)/shard_map/reduce_scatter | solution.py:33
Sparse Core Ops, SparseCore 0:
  10.2 40.5 all-gather.1
  57.8 10.7 reduce-scatter.2
  83.1 98.0 all-reduce.1
  190.5 11.2 reduce-scatter.4
where the time goes:
time: 250 us
  waiting for transfers between devices  164 us (66%)
  matrix products  38.2 us (15%)
  blocking collectives  16.9 us (7%)
  between operations  13.8 us (6%)
  local copies, waits for them, and re-layouts  11.8 us (5%)
  other arithmetic  4.72 us (2%)
    psum x1, waiting for transfers between devices, on_device(): summed = lax.psum(recon_terms, 'lat')  98.1 us
    all_gather x1, waiting for transfers between devices, on_device(): whole_rows = lax.all_gather(acts, 'lat', axis=1, tiled=True)  42.8 us
    unnamed x9, local copies, waits for them, and re-layouts  11.8 us
    reduce_scatter x1, waiting for transfers between devices, on_device(): lax.psum_scatter(backed.astype(jnp.bfloat16), 'feat', scatter_dimension=0...  11.4 us
    reduce_scatter x1, waiting for transfers between devices, on_device(): lax.psum_scatter(partial_value.astype(jnp.bfloat16), 'feat', scatter_dime...  10.8 us
    dot_general x1, matrix products, on_device(): jnp.einsum('mrd,rl->mdl', resid_rows, latents, preferred_element_type=jnp...  9.21 us
    dot_general x1, matrix products, on_device(): jnp.einsum('mrd,rl->mdl', whole_rows, grad_pre_b, preferred_element_type=...  8.09 us
    dot_general x1, matrix products, on_device(): jnp.einsum('rl,mdl->mrd', latents, weight, preferred_element_type=jnp.flo...  7.56 us
  transfers between devices with their start and end apart: 4, of which 4 were waited for; matrix products, arithmetic and copies ran while one was open for 0% of the time, Pallas kernels for 0%

commit v1 on v0

--- a/solution.py
+++ b/solution.py
@@ -25,7 +25,9 @@
     act_share = jax.nn.softplus(pre_share).astype(jnp.bfloat16)
     latents = lax.all_gather(act_share, "feat", axis=0, tiled=True)
     recon_terms = jnp.einsum("rl,mdl->mrd", latents, weight, preferred_element_type=jnp.float32)
-    summed = lax.psum(recon_terms, "lat")
+    summed = recon_terms
+    for hop in (1, 2, 4, 8):
+        summed = summed + lax.ppermute(summed, "lat", [(dev, dev ^ hop) for dev in range(16)])
     resid = scale * summed + dec_bias[:, None, :] - whole_rows.astype(jnp.float32)
     grad_dec_bias = jnp.sum(resid, axis=1)
     resid_rows = resid.astype(jnp.bfloat16)

time: 250 us -> 337 us (1.35)
  waiting for transfers between devices: 164 us -> 251 us
  matrix products: 38.2 us -> 32.5 us
  starting transfers between devices: 0.16 us -> 5.76 us
    ppermute x0 -> x4, waiting for transfers between devices: none -> 185 us  [on_device(): lax.ppermute(summed, 'lat', [(dev, dev ^ hop) for dev in range(16)])]
    psum x1 -> x0, waiting for transfers between devices: 98.1 us -> none  [on_device(): summed = lax.psum(recon_terms, 'lat')]
    ppermute x0 -> x4, starting transfers between devices: none -> 5.64 us  [on_device(): lax.ppermute(summed, 'lat', [(dev, dev ^ hop) for dev in range(16)])]
    unnamed x9 -> x13, local copies, waits for them, and re-layouts: 11.8 us -> 11.9 us
  transfers between devices with their start and end apart: 4 -> 7, of which waited for: 4 -> 7; matrix products, arithmetic and copies ran while one was open for 0% -> 0% of each run, Pallas kernels for 0% -> 0%
where the time goes in v1:
time: 337 us
  waiting for transfers between devices  251 us (74%)
  matrix products  32.5 us (10%)
  blocking collectives  16.9 us (5%)
  between operations  13.8 us (4%)
  local copies, waits for them, and re-layouts  11.9 us (4%)
  starting transfers between devices  5.76 us (2%)
  other arithmetic  4.33 us (1%)
    ppermute x4, waiting for transfers between devices, on_device(): lax.ppermute(summed, 'lat', [(dev, dev ^ hop) for dev in range(16)])  185 us
    all_gather x1, waiting for transfers between devices, on_device(): whole_rows = lax.all_gather(acts, 'lat', axis=1, tiled=True)  42.8 us
    reduce_scatter x1, waiting for transfers between devices, on_device(): lax.psum_scatter(backed.astype(jnp.bfloat16), 'feat', scatter_dimension=0...  11.9 us
    unnamed x13, local copies, waits for them, and re-layouts  11.9 us
    reduce_scatter x1, waiting for transfers between devices, on_device(): lax.psum_scatter(partial_value.astype(jnp.bfloat16), 'feat', scatter_dime...  10.8 us
    dot_general x1, matrix products, on_device(): jnp.einsum('mrd,rl->mdl', resid_rows, latents, preferred_element_type=jnp...  9.22 us
    dot_general x1, matrix products, on_device(): jnp.einsum('mrd,rl->mdl', whole_rows, grad_pre_b, preferred_element_type=...  8.11 us
  transfers between devices with their start and end apart: 7, of which 7 were waited for; matrix products, arithmetic and copies ran while one was open for 0% of the time, Pallas kernels for 0%

profile of v1, /device:TPU:0, one launch (start us, length us, event | category | flops | bytes accessed | tf_op | source)
XLA Modules:
  0.0 336.5 jit_solution(15866853445695223058)
XLA Ops:
  7.2 0.0 all-gather.2.cloned.1.call-start
  7.2 0.7 all-gather.2.cloned.1.call-update
  7.9 0.0 reduce-scatter.3.cloned.1.call-start
  7.9 42.8 %all-gather.2.cloned.1.call-done = bf16[2,128,2048]{2,1,0:T(8,128)(2,1)} async-done(((bf16[2,8,2048]{2,1,0:T(8,128)(2,1)}), bf16[2,128,2048]{2,1,0:T(8,128)(2,1)}) %all-gather.2.cloned.1.call-update) | async-done | bytes 1048592 | tf_op jit(solution)/shard_map/all_gather | solution.py:17
  50.8 0.0 copy-start
  50.8 3.1 fusion.3
  53.9 0.0 copy-done
  53.9 0.0 copy-start.3
  53.9 3.6 %fusion.22 = bf16[128,1024]{1,0:T(8,128)(2,1)} fusion(f32[128,1024]{1,0:T(8,128)S(1)} %fusion.3, bf16[2,2048,1024]{2,1,0:T(8,128)(2,1)} %param.5, bf16[2,128,2048]{2,1,0:T(8,128)(2,1)S(1)} %copy-done), kind=kOutput, calls=%fused_computation.19 | convolution fusion | flops 537133056 | bytes 5505024 | tf_op jit(solution)/shard_map/dot_general | solution.py:9
  57.6 0.0 reduce-scatter.3.cloned.1.call-update
  57.6 0.0 reduce-scatter.5.cloned.1.call-start
  57.6 10.8 %reduce-scatter.3.cloned.1.call-done = bf16[64,1024]{1,0:T(8,128)(2,1)} async-done(((bf16[128,1024]{1,0:T(8,128)(2,1)}), bf16[64,1024]{1,0:T(8,128)(2,1)}) %reduce-scatter.3.cloned.1.call-update) | async-done | bytes 131088 | tf_op jit(solution)/shard_map/reduce_scatter | solution.py:20
  68.5 0.0 copy-done.3
  68.5 1.1 fusion.25
  69.6 5.7 %all_gather.10 = bf16[128,1024]{1,0:T(8,128)(2,1)S(1)} all-gather(bf16[64,1024]{1,0:T(8,128)(2,1)S(1)} %fusion.25), channel_id=1, replica_groups=mesh['feat'=2,'lat'=16] {'feat'}, dimensions={0}, use_global_device_ids=true | all-gather | bytes 393216 | tf_op jit(solution)/shard_map/all_gather | solution.py:26
  75.3 6.2 %convolution_bitcast_fusion = f32[2,128,2048]{2,1,0:T(8,128)S(1)} fusion(bf16[2,2048,1024]{2,1,0:T(8,128)(2,1)} %param.5, bf16[128,1024]{1,0:T(8,128)(2,1)S(1)} %all_gather.10), kind=kOutput, calls=%fused_computation.14 | convolution fusion | flops 1073741824 | bytes 10747904 | tf_op jit(solution)/shard_map/rl,mdl->mrd/dot_general | solution.py:27
  81.5 0.1 collective-permute-start
  81.6 4.1 %collective-permute-done = f32[2,128,2048]{2,1,0:T(8,128)S(1)} collective-permute-done((f32[2,128,2048]{2,1,0:T(8,128)S(1)}, f32[2,128,2048]{2,1,0:T(8,128)S(1)}, u32[]{:S(2)}, u32[]{:S(2)}) %collective-permute-start) | collective-permute-done | bytes 2097184 | tf_op jit(solution)/shard_map/ppermute | solution.py:30
  85.7 0.3 add.54
  86.1 1.5 collective-permute-start.1
  87.6 46.2 %collective-permute-done.1 = f32[2,128,2048]{2,1,0:T(8,128)S(1)} collective-permute-done((f32[2,128,2048]{2,1,0:T(8,128)S(1)}, f32[2,128,2048]{2,1,0:T(8,128)S(1)}, u32[]{:S(2)}, u32[]{:S(2)}) %collective-permute-start.1) | collective-permute-done | bytes 2097184 | tf_op jit(solution)/shard_map/ppermute | solution.py:30
  133.8 0.0 slice-start
  133.8 0.3 add.55
  134.2 0.0 copy-start.2
  134.2 0.0 slice-start.1
  134.2 1.6 collective-permute-start.2
  135.8 45.3 %collective-permute-done.2 = f32[2,128,2048]{2,1,0:T(8,128)S(1)} collective-permute-done((f32[2,128,2048]{2,1,0:T(8,128)S(1)}, f32[2,128,2048]{2,1,0:T(8,128)S(1)}, u32[]{:S(2)}, u32[]{:S(2)}) %collective-permute-start.2) | collective-permute-done | bytes 2097184 | tf_op jit(solution)/shard_map/ppermute | solution.py:30
  181.1 0.3 add.56
  181.4 2.5 collective-permute-start.3
  183.9 89.4 %collective-permute-done.3 = f32[2,128,2048]{2,1,0:T(8,128)S(1)} collective-permute-done((f32[2,128,2048]{2,1,0:T(8,128)S(1)}, f32[2,128,2048]{2,1,0:T(8,128)S(1)}, u32[]{:S(2)}, u32[]{:S(2)}) %collective-permute-start.3) | collective-permute-done | bytes 2097184 | tf_op jit(solution)/shard_map/ppermute | solution.py:30
  273.3 0.0 copy-done.2
  273.3 1.2 fusion.30
  274.5 0.0 slice-done
  274.5 0.0 slice-done.1
  274.5 0.7 fusion.1
  275.3 0.0 copy-start.1
  275.3 1.5 fusion.19
  276.8 0.0 reduce-scatter.5.cloned.1.call-update
  276.8 11.9 %reduce-scatter.5.cloned.1.call-done = bf16[64,1024]{1,0:T(8,128)(2,1)} async-done(((bf16[128,1024]{1,0:T(8,128)(2,1)}), bf16[64,1024]{1,0:T(8,128)(2,1)}) %reduce-scatter.5.cloned.1.call-update) | async-done | bytes 131088 | tf_op jit(solution)/shard_map/reduce_scatter | solution.py:35
  288.7 0.0 copy-done.1
  288.7 1.0 fusion.32
  289.7 5.5 %psum.7 = f32[1024]{0:T(1024)} all-reduce(f32[1024]{0:T(1024)S(1)} %get-tuple-element.8), channel_id=1, replica_groups=mesh['feat'=2,'lat'=16] {'feat'}, use_global_device_ids=true, to_apply=%region_3.4 | all-reduce | flops 1024 | bytes 8192 | tf_op jit(solution)/shard_map/psum | solution.py:39
  295.2 5.6 %all_gather.11 = bf16[128,1024]{1,0:T(8,128)(2,1)S(1)} all-gather(bf16[64,1024]{1,0:T(8,128)(2,1)S(1)} %get-tuple-element.9), channel_id=1, replica_groups=mesh['feat'=2,'lat'=16] {'feat'}, dimensions={0}, use_global_device_ids=true | all-gather | bytes 393216 | tf_op jit(solution)/shard_map/all_gather | solution.py:40
  300.9 8.1 %fusion.26 = f32[1024,2,2048]{2,0,1:T(8,128)} fusion(bf16[2,128,2048]{2,1,0:T(8,128)(2,1)S(1)} %copy-done, bf16[128,1024]{1,0:T(8,128)(2,1)S(1)} %all_gather.11), kind=kOutput, calls=%fused_computation.26 | convolution fusion | flops 1073741824 | bytes 18087936 | tf_op jit(solution)/shard_map/mrd,rl->mdl/dot_general | solution.py:41
  309.0 9.2 %fusion = bf16[2,2048,1024]{1,2,0:T(8,128)(2,1)} fusion(f32[1024,2,2048]{2,0,1:T(8,128)} %fusion.26, bf16[2,128,2048]{2,1,0:T(8,128)(2,1)S(1)} %get-tuple-element.7, bf16[128,1024]{1,0:T(8,128)(2,1)S(1)} %all_gather.10), kind=kOutput, calls=%fused_computation.1 | convolution fusion | flops 1086324736 | bytes 26476544 | tf_op jit(solution)/shard_map/mrd,rl->mdl/dot_general | solution.py:42
  318.2 11.8 %copy.9 = bf16[2,2048,1024]{2,1,0:T(8,128)(2,1)} copy(bf16[2,2048,1024]{1,2,0:T(8,128)(2,1)} %fusion) | data formatting | bytes 16777216
  (1 shorter events, 0.0 us)
Async XLA Ops:
  7.2 43.6 %all-gather.2.cloned.1.call-start = ((), (), s32[]{:S(2)}) async-start(), calls=%async_computation.2 | async-start | bytes 1114112 | tf_op jit(solution)/shard_map/all_gather | solution.py:17
  7.9 60.6 %reduce-scatter.3.cloned.1.call-start = ((), (), s32[]{:S(2)}) async-start(), calls=%async_computation.3 | async-start | bytes 393216 | tf_op jit(solution)/shard_map/reduce_scatter | solution.py:20
  50.8 3.2 copy-start
  53.9 14.5 %copy-start.3 = (f32[1024]{0:T(1024)S(1)}, f32[1024]{0:T(1024)}, u32[]{:S(2)}) copy-start(f32[1024]{0:T(1024)} %param.6) | copy-start | bytes 12292
  57.6 231.1 %reduce-scatter.5.cloned.1.call-start = ((), (), s32[]{:S(2)}) async-start(), calls=%async_computation.4 | async-start | bytes 393216 | tf_op jit(solution)/shard_map/reduce_scatter | solution.py:35
  81.5 4.2 %collective-permute-start = (f32[2,128,2048]{2,1,0:T(8,128)S(1)}, f32[2,128,2048]{2,1,0:T(8,128)S(1)}, u32[]{:S(2)}, u32[]{:S(2)}) collective-permute-start(f32[2,128,2048]{2,1,0:T(8,128)S(1)} %convolution_bitcast_fusion), channel_id=1, source_target_pairs={{0,1},{1,0},{2,3},{3,2},{4,5},{5,4},{6,7},{7,6},{8,9},{9,8},{10,11... | collective-permute-start | bytes 6291464 | tf_op jit(solution)/shard_map/ppermute | solution.py:30
  86.1 47.7 %collective-permute-start.1 = (f32[2,128,2048]{2,1,0:T(8,128)S(1)}, f32[2,128,2048]{2,1,0:T(8,128)S(1)}, u32[]{:S(2)}, u32[]{:S(2)}) collective-permute-start(f32[2,128,2048]{2,1,0:T(8,128)S(1)} %add.54), channel_id=1, source_target_pairs={{0,2},{1,3},{2,0},{3,1},{4,6},{5,7},{6,4},{7,5},{8,10},{9,11},{10,... | collective-permute-start | bytes 6291464 | tf_op jit(solution)/shard_map/ppermute | solution.py:30
  133.8 140.7 %slice-start = ((s8[8388608]{0:T(1024)(128)(4,1)}), s8[4194304]{0:T(1024)(128)(4,1)S(1)}, s32[]{:S(2)}) async-start(s8[8388608]{0:T(1024)(128)(4,1)} %bitcast.47), calls=%async_computation.5 | async-start | bytes 8388608
  134.2 139.1 %copy-start.2 = (f32[2,2048]{1,0:T(2,128)S(1)}, f32[2,2048]{1,0:T(2,128)}, u32[]{:S(2)}) copy-start(f32[2,2048]{1,0:T(2,128)} %param.7) | copy-start | bytes 49156
  134.2 140.4 %slice-start.1 = ((s8[8388608]{0:T(1024)(128)(4,1)}), s8[4194304]{0:T(1024)(128)(4,1)S(1)}, s32[]{:S(2)}) async-start(s8[8388608]{0:T(1024)(128)(4,1)} %bitcast.47), calls=%async_computation.6 | async-start | bytes 8388608
  134.2 46.9 %collective-permute-start.2 = (f32[2,128,2048]{2,1,0:T(8,128)S(1)}, f32[2,128,2048]{2,1,0:T(8,128)S(1)}, u32[]{:S(2)}, u32[]{:S(2)}) collective-permute-start(f32[2,128,2048]{2,1,0:T(8,128)S(1)} %add.55), channel_id=1, source_target_pairs={{0,4},{1,5},{2,6},{3,7},{4,0},{5,1},{6,2},{7,3},{8,12},{9,13},{10,... | collective-permute-start | bytes 6291464 | tf_op jit(solution)/shard_map/ppermute | solution.py:30
  181.4 91.9 %collective-permute-start.3 = (f32[2,128,2048]{2,1,0:T(8,128)S(1)}, f32[2,128,2048]{2,1,0:T(8,128)S(1)}, u32[]{:S(2)}, u32[]{:S(2)}) collective-permute-start(f32[2,128,2048]{2,1,0:T(8,128)S(1)} %add.56), channel_id=1, source_target_pairs={{0,8},{1,9},{2,10},{3,11},{4,12},{5,13},{6,14},{7,15},{8,0},{9,1},... | collective-permute-start | bytes 6291464 | tf_op jit(solution)/shard_map/ppermute | solution.py:30
  275.3 13.4 %copy-start.1 = (bf16[64,1024]{1,0:T(8,128)(2,1)S(1)}, bf16[64,1024]{1,0:T(8,128)(2,1)}, u32[]{:S(2)}) copy-start(bf16[64,1024]{1,0:T(8,128)(2,1)} %reduce-scatter.3.cloned.1.call-done) | copy-start | bytes 393220
Sparse Core Ops, SparseCore 0:
  10.2 40.5 all-gather.1
  57.7 10.7 reduce-scatter.2
  276.9 11.7 reduce-scatter.4
